TPU v7x, 32 devices: a whole 2x2x4 slice. The times are simulated.
32 devices in a mesh: seq: 8 (over z, y), ffn: 4 (over x, core).
Axes of the slice: x: 2, y: 2, z: 4, core: 2. Of those that a mesh axis runs over, the one named last changes fastest.
Arguments:
- child_feat: bfloat16 [4096, 1024], P('seq'), may hold values from -6 to 6
- parent_feat: bfloat16 [512, 1024], P('seq'), may hold values from -6 to 6
- child_parent: int32 [4096], P('seq'), may hold values from 0 to 63
- owner: int32 [4096, 1], P('seq'), may hold values from 0 to 7; in each aligned block of 512 rows (0 to 511, 512 to 1023, ...) at most 128 rows name the same one
- log_gate: float32 [16, 8192], P('ffn', 'seq'), may hold values from -1 to 0
- norm_gain: bfloat16 [1024], replicated, may hold values from 0.3984375 to 1.59375
- w_query: bfloat16 [1024, 1024], P(None, 'ffn'), may hold values from -0.1875 to 0.1875
- w_key: bfloat16 [1024, 1024], P(None, 'ffn'), may hold values from -0.1875 to 0.1875
- w_value: bfloat16 [1024, 1024], P(None, 'ffn'), may hold values from -0.1875 to 0.1875
- head_gain: bfloat16 [1024], P('ffn'), may hold values from 0.25 to 1.75
- w_out: bfloat16 [1024, 1024], P('ffn'), may hold values from -0.1875 to 0.1875
- ffn_gain: bfloat16 [1024], replicated, may hold values from 0.3984375 to 1.59375
- w_up: bfloat16 [1024, 4096], P(None, 'ffn'), may hold values from -0.1875 to 0.1875
- w_down: bfloat16 [4096, 1024], P('ffn'), may hold values from -0.09375 to 0.09375
Outputs:
- child_out: bfloat16 [4096, 1024], P('seq', 'ffn')
Inputs may be any that keep to these rules, and one draw needn't show every extreme that they name: The parent of child i is row (i // 512) * 64 + child_parent[i] of parent_feat. Among the 512 children of one index of seq, at most 128 name the same owner, and in every draw some owner is named exactly 128 times by some block.
All inputs are finite; a program needn't handle non-finite values.
Results may differ from a plain program's by a relative error of at most 0.013.
Values may be sent and summed in bfloat16 or wider, within the bound.
No kernel may reach another device: no remote copies, remote signals or barrier semaphores. Data moves between devices by JAX's collectives and lax.ppermute only.
A program may use at most 64 MiB of HBM per device.

v0:
```python
import functools

import jax
import jax.numpy as jnp
from jax import lax
from jax.experimental import pallas as pl
from jax.experimental.pallas import tpu as pltpu
from jax.sharding import PartitionSpec as P


EPSILON = 1e-05
F32 = jnp.float32
BF16 = jnp.bfloat16
LANES = 128
SPLIT = 12
NT = (((1,), (1,)), ((), ()))
TN = (((0,), (0,)), ((), ()))
VMEM = pl.BlockSpec(memory_space=pltpu.VMEM)
HBM = pl.BlockSpec(memory_space=pltpu.HBM)


def split3(values):
    high = values.astype(BF16)
    rest = values - high.astype(F32)
    middle = rest.astype(BF16)
    low = (rest - middle.astype(F32)).astype(BF16)
    return high, middle, low


def dot(a, b):
    return jnp.dot(a, b, preferred_element_type=F32)


def iota(shape, dim):
    return lax.broadcasted_iota(jnp.int32, shape, dim)


def row_norm(values, scales):
    return values * lax.rsqrt(jnp.mean(values * values, axis=-1, keepdims=True) + EPSILON) * scales


def column(row, width=LANES):
    return jnp.broadcast_to(row, (width, row.shape[1])).T


def head_of_lane(shape, hd):
    return iota(shape, len(shape) - 1) // hd


def fetch(pairs, sems):
    copies = [pltpu.make_async_copy(src, dst, sems.at[i]) for i, (src, dst) in enumerate(pairs)]
    for copy in copies:
        copy.start()
    return copies


def pre_kernel(
    cap, blocks, cf, pf, pick, own, gain, wq, wk, wv,
    joined, q, k, v, taken, own_out,
    cf_v, pf_v, pick_v, own_v, gain_v, w_v, joined_v, sems, out_sems,
):
    tokens = cf.shape[0]
    parents = pf.shape[0]
    tile = min(256, tokens)
    starts = range(0, tokens, tile)
    small = fetch(
        [(own, own_v), (pick, pick_v), (pf, pf_v), (gain, gain_v)]
        + [(cf.at[pl.ds(at, tile)], cf_v.at[pl.ds(at, tile)]) for at in starts]
        + [(w, w_v.at[i]) for i, w in enumerate((wq, wk, wv))],
        sems,
    )
    parts, weights = small[4 : 4 + len(starts)], small[4 + len(starts) :]
    small[0].wait()
    owners = own_v[...]
    own_out[...] = owners
    lane = iota((1, blocks * cap), 1)
    lane_owner, lane_rank = lane // cap, lane % cap
    ones = jnp.ones((tokens, LANES), BF16)
    for at in starts:
        rows = pl.ds(at, tile)
        mine = column(own_v[:, rows])
        same = (mine[:, :1] == owners) & (iota((tile, tokens), 0) + at >= iota((tile, tokens), 1))
        count = dot(jnp.where(same, 1.0, 0.0).astype(BF16), ones)
        rank = count[:, :1].astype(jnp.int32) - 1
        kept = (mine[:, :1] == lane_owner) & (lane_rank <= rank)
        taken[rows, :] = jnp.where(kept, 1.0, 0.0).astype(BF16)
    for copy in small[1:4]:
        copy.wait()
    scales = gain_v[...].astype(F32).reshape(1, -1)
    stores = []
    for i, at in enumerate(starts):
        rows = pl.ds(at, tile)
        parts[i].wait()
        chosen = jnp.where(iota((parents, tile), 0) == pick_v[:, rows], 1.0, 0.0).astype(BF16)
        added = lax.dot_general(chosen, pf_v[...], TN, preferred_element_type=F32)
        summed = (cf_v[rows, :].astype(F32) + added).astype(BF16)
        joined_v[rows, :] = summed
        store = pltpu.make_async_copy(joined_v.at[rows], joined.at[rows], out_sems.at[i])
        store.start()
        stores.append(store)
        normed = row_norm(summed.astype(F32), scales).astype(BF16)
        if i == 0:
            for copy in weights:
                copy.wait()
        for j, out in enumerate((q, k, v)):
            out[rows, :] = dot(normed, w_v[j]).astype(BF16)
    for store in stores:
        store.wait()


def gate_rows(gates, blocks):
    if len(gates.shape) == 3:
        rows = jnp.concatenate([gates[o] for o in range(blocks)], axis=1)
    else:
        rows = gates[...]
    heads = rows.shape[0]
    rows = jnp.concatenate([rows, jnp.zeros((8 - heads, rows.shape[1]), F32)], axis=0)
    return jnp.concatenate([part.astype(F32) for part in split3(rows)], axis=0).astype(BF16)


def seat(owner, blocks):
    half = max(blocks // 2, 1)
    return owner // half * (8 * pl.cdiv(half, 8)) + owner % half


def put_tail(send, decay, at):
    high = decay.astype(BF16)
    low = decay - high.astype(F32)
    send[at:, :] = jnp.concatenate([high.astype(F32), low], axis=0).astype(BF16)


def state_kernel(cap, blocks, hd, taken, gates, k, v, own, c_lanes, c_rows, *outs):
    tokens, share = k.shape
    half = blocks // 2
    rows = 8 * pl.cdiv(half, 8)
    table = gate_rows(gates, blocks)
    slots = table.shape[1]
    summed = lax.dot_general(taken[...], table, NT, preferred_element_type=F32)
    lanes = LANES * pl.cdiv(2 * rows, LANES)
    chunk = jnp.where(
        seat(iota((slots, lanes), 0) // cap, blocks) == iota((slots, lanes), 1), 1.0, 0.0
    ).astype(BF16)
    totals = dot(table, chunk)
    totals = jnp.concatenate(
        [part.astype(F32) for part in split3(totals[:8] + totals[8:16] + totals[16:])], axis=0
    ).astype(BF16)
    mine = column(seat(own[...], blocks))[:, :1]
    named = jnp.where(mine == iota((tokens, lanes), 1), 1.0, 0.0).astype(BF16)
    whole = lax.dot_general(named, totals, NT, preferred_element_type=F32)
    summed = jnp.concatenate([summed, whole], axis=0)
    spread = jnp.where(
        iota((24, share), 0) % 8 == head_of_lane((24, share), hd), 1.0, 0.0
    ).astype(BF16)
    wide = sum(dot(part, spread) for part in split3(summed))
    c_lanes[...] = wide[:tokens]
    turned_c = lax.dot_general(table, taken[...], NT, preferred_element_type=F32)
    c_rows[...] = turned_c[:8] + turned_c[8:16] + turned_c[16:]
    faded = k[...].astype(F32) * jnp.exp(jnp.minimum(wide[tokens:] - wide[:tokens], 0.0))
    turned = faded.astype(BF16).T
    decays = jnp.exp(lax.dot_general(totals, spread, TN, preferred_element_type=F32))
    owners = own[...]
    values = v[...]
    lane_head = head_of_lane((hd, share), hd)
    for g in range(2):
        send, state, decay = outs[3 * g : 3 * g + 3]

        def one(i, nothing):
            masked = jnp.where(owners == i + g * half, turned, jnp.zeros_like(turned))
            full = dot(masked, values)
            packed = jnp.zeros((hd, share), F32)
            for h in range(share // hd):
                packed = jnp.where(lane_head == h, full[h * hd : (h + 1) * hd], packed)
            state[i] = packed
            send[pl.ds(pl.multiple_of(i * hd, hd), hd), :] = packed.astype(BF16)
            return nothing

        lax.fori_loop(0, half, one, 0, unroll=blocks <= 8)
        decay[...] = decays[g * rows : (g + 1) * rows]
        put_tail(send, decay[...], half * hd)


def joined_scan(bit, hd, refs):
    came, state, decay, prefix, lead = refs
    half = state.shape[0]
    rows = decay.shape[0]
    upper = ((lax.axis_index("seq") & bit) // bit).astype(F32)
    tail = came[half * hd :, :].astype(F32)
    theirs_decay = tail[:rows] + tail[rows:]
    mine_decay = decay[...]
    past = jnp.ones_like(mine_decay) if lead is None else lead[...]
    scale_mine = upper + (1.0 - upper) * theirs_decay
    scale_theirs = upper * mine_decay + (1.0 - upper)
    add = upper * past
    pairs = []
    for i in range(half):
        theirs = came[i * hd : (i + 1) * hd, :].astype(F32)
        total = scale_mine[i : i + 1] * state[i] + scale_theirs[i : i + 1] * theirs
        before = add[i : i + 1] * theirs
        pairs.append((total, before if prefix is None else prefix[i] + before))
    return pairs, mine_decay * theirs_decay, past * scale_mine_lead(upper, theirs_decay)


def scale_mine_lead(upper, theirs_decay):
    return upper * theirs_decay + (1.0 - upper)


def step_kernel(bit, hd, first, *refs):
    came, state, decay = refs[:3]
    prefix, lead = (None, None) if first else refs[3:5]
    send, state_out, decay_out, prefix_out, lead_out = refs[-5:]
    pairs, total_decay, total_lead = joined_scan(bit, hd, (came, state, decay, prefix, lead))
    for i, (total, before) in enumerate(pairs):
        state_out[i] = total
        prefix_out[i] = before
        send[i * hd : (i + 1) * hd, :] = total.astype(BF16)
    decay_out[...] = total_decay
    lead_out[...] = total_lead
    put_tail(send, total_decay, len(pairs) * hd)


def inside_kernel(hd, q, k, v, c_lanes, c_rows, own, inside):
    tokens, share = q.shape
    heads = share // hd
    tile = min(256, tokens)
    for at in range(0, tokens, tile):
        rows = pl.ds(at, tile)
        reach = at + tile
        mine = column(own[:, rows])[:, :1]
        same = (mine == own[:, :reach]) & (
            iota((tile, reach), 0) + at >= iota((tile, reach), 1)
        )
        queries = q[rows, :]
        keys = k[:reach, :]
        values = v[:reach, :]
        total = jnp.zeros((tile, share), F32)
        for h in range(heads):
            only = head_of_lane((tile, share), hd) == h
            scores = lax.dot_general(
                jnp.where(only, queries, jnp.zeros_like(queries)),
                keys,
                NT,
                preferred_element_type=F32,
            )
            gap = c_lanes[rows, h * hd : h * hd + 1] - c_rows[h : h + 1, :reach]
            decay = jnp.where(same, jnp.exp(jnp.where(same, gap, 0.0)), 0.0)
            mixing = (scores * decay).astype(BF16)
            only = head_of_lane((reach, share), hd) == h
            total += dot(mixing, jnp.where(only, values, jnp.zeros_like(values)))
        inside[rows, :] = total


def outside_kernel(bit, owners, hd, *refs):
    pairs, whole, lead = joined_scan(bit, hd, refs[:5])
    q, own, *refs = refs[5:]
    carry = jnp.zeros(pairs[0][0].shape, F32) if owners[0] == 0 else refs.pop(0)[...]
    _, share = q.shape
    heads = share // hd
    mine = column(own[...])[:, :1]
    queries = q[...]
    block_diagonal = iota((share, share), 0) // hd == iota((share, share), 1) // hd
    wide, table = refs[-2:]
    for i, (total, before) in enumerate(pairs):
        state = before + lead[i : i + 1] * carry
        stacked = jnp.concatenate([state] * heads, axis=0)
        at = pl.ds(i * share, share)
        table[at, :] = jnp.where(block_diagonal, stacked, 0.0).astype(BF16)
        wide[:, at] = jnp.where(mine == owners[i], queries, jnp.zeros_like(queries))
        carry = whole[i : i + 1] * carry + total
    outside = dot(wide[...], table[...])
    if owners[0] == 0:
        part, carried = refs[:2]
        part[...] = outside
        carried[...] = carry
        return
    earlier, c_lanes, inside, gain, both, first, second = refs[:7]
    combined = inside[...] + (outside + earlier[...]) * jnp.exp(c_lanes[...])
    square = combined * combined
    mean = jnp.where(block_diagonal, 1.0 / hd, 0.0).astype(BF16)
    spread = sum(dot(part, mean) for part in split3(square))
    flat = (combined * lax.rsqrt(spread + EPSILON) * gain[...].astype(F32)).astype(BF16)
    both[...] = flat
    first[...] = flat[: first.shape[0]]
    second[...] = flat[first.shape[0] :]


def fetch_kernel(*refs):
    sources, gain, outs, (scale, gain_v, sems) = refs[:4], refs[4], refs[5:9], refs[9:]
    copies = fetch([(gain, gain_v), *zip(sources, outs)], sems)
    copies[0].wait()
    scale[...] = gain_v[...].astype(F32).reshape(1, -1)
    for copy in copies[1:]:
        copy.wait()


def own_kernel(mine, near, own_w, near_w, joined, hidden):
    tokens = joined.shape[0]
    tile = min(256, tokens)
    for at in range(0, tokens, tile):
        rows = pl.ds(at, tile)
        hidden[rows, :] = (
            joined[rows, :].astype(F32)
            + dot(mine[rows, :], own_w[...])
            + dot(near[rows, :], near_w[...])
        )


def ffn_kernel(groups, at, *refs):
    flats, wouts = refs[: groups - 2], refs[groups - 2 : 2 * (groups - 2)]
    hidden_v, scale, up_v, down_v, own, even, odd, scratch = refs[2 * (groups - 2) :]
    mine = lax.axis_index("ffn")
    rows, cols = own.shape
    hidden = hidden_v[pl.ds(at, rows), :]
    for flat, wout in zip(flats, wouts):
        hidden = hidden + dot(flat[...], wout[...])
    scratch[...] = hidden
    second = row_norm(hidden, scale[...]).astype(BF16)
    expanded = jax.nn.gelu(dot(second, up_v[...])).astype(BF16)
    for j in sorted(range(groups), key=lambda j: -(j % 2)):
        target = pl.ds(pl.multiple_of((mine ^ j) * cols, cols), cols)
        piece = dot(expanded, down_v[:, target])
        if j == 0:
            own[...] = piece + scratch[:, target]
        elif j % 2:
            odd[:, pl.ds((j // 2) * cols, cols)] = piece.astype(BF16)
        else:
            even[:, pl.ds((j // 2 - 1) * cols, cols)] = piece


def final_kernel(*refs):
    out = refs[-1]
    at = 0
    for i in range(2):
        own, near, far = refs[3 * i : 3 * i + 3]
        rows, cols = own.shape
        place = pl.ds(at, rows)
        at += rows
        out[place, :] = (
            own[...] + near[:, :cols].astype(F32) + far[...].astype(F32)
        ).astype(BF16)


def flip(array, axis, bit):
    size = lax.axis_size(axis)
    return lax.ppermute(array, axis, [(i, i ^ bit) for i in range(size)])


def gather_flips(array, axis):
    size = lax.axis_size(axis)
    parts = {0: array}
    bit = size // 2
    while bit:
        for k in list(parts):
            parts[k ^ bit] = flip(parts[k], axis, bit)
        bit //= 2
    return [parts[k] for k in range(size)]


def grant(mebibytes):
    return pltpu.CompilerParams(vmem_limit_bytes=mebibytes << 20)


def shaped(shape, dtype):
    return jax.ShapeDtypeStruct(shape, dtype)


def in_hbm(array):
    return pltpu.with_memory_space_constraint(array, pltpu.HBM)


def exchange(array):
    return lax.all_to_all(array, "seq", split_axis=0, concat_axis=0, tiled=True)


def on_device(
    child_feat,
    parent_feat,
    child_parent,
    owner,
    log_gate,
    norm_gain,
    w_query,
    w_key,
    w_value,
    head_gain,
    w_out,
    ffn_gain,
    w_up,
    w_down,
):
    blocks = lax.axis_size("seq")
    groups = lax.axis_size("ffn")
    heads, slots = log_gate.shape
    cap = slots // blocks
    tokens, width = child_feat.shape
    share = w_query.shape[1]
    hd = share // heads
    cols = width // groups

    child_feat, parent_feat, w_query, w_key, w_value, w_up, w_down = map(
        in_hbm, (child_feat, parent_feat, w_query, w_key, w_value, w_up, w_down)
    )
    arrived = exchange(log_gate.reshape(heads, blocks, cap).transpose(1, 0, 2))
    if cap % LANES:
        arrived = arrived.transpose(1, 0, 2).reshape(heads, slots)
    wout_parts = gather_flips(w_out, "ffn")

    tiles = pl.cdiv(tokens, min(256, tokens))
    joined, q, k, v, taken, own = pl.pallas_call(
        functools.partial(pre_kernel, cap, blocks),
        out_shape=(
            pltpu.HBM((tokens, width), BF16),
            shaped((tokens, share), BF16),
            shaped((tokens, share), BF16),
            shaped((tokens, share), BF16),
            shaped((tokens, slots), BF16),
            shaped((1, tokens), jnp.int32),
        ),
        in_specs=[HBM] * 8,
        out_specs=[HBM] + [VMEM] * 5,
        scratch_shapes=[
            pltpu.VMEM((tokens, width), BF16),
            pltpu.VMEM(parent_feat.shape, BF16),
            pltpu.VMEM((1, tokens), jnp.int32),
            pltpu.VMEM((1, tokens), jnp.int32),
            pltpu.VMEM((width,), BF16),
            pltpu.VMEM((3, width, share), BF16),
            pltpu.VMEM((tokens, width), BF16),
            pltpu.SemaphoreType.DMA((7 + tiles,)),
            pltpu.SemaphoreType.DMA((tiles,)),
        ],
        name="pre",
        compiler_params=grant(20),
    )(
        child_feat,
        parent_feat,
        in_hbm(child_parent.reshape(1, tokens)),
        in_hbm(owner.reshape(1, tokens)),
        in_hbm(norm_gain),
        w_query,
        w_key,
        w_value,
    )

    half = blocks // 2
    seats = 8 * pl.cdiv(half, 8)
    sent = shaped((half * hd + 2 * seats, share), BF16)
    held = shaped((half, hd, share), F32)
    rate = shaped((seats, share), F32)
    c_lanes, c_rows, *made = pl.pallas_call(
        functools.partial(state_kernel, cap, blocks, hd),
        out_shape=(shaped((tokens, share), F32), shaped((8, tokens), F32)) + (sent, held, rate) * 2,
        in_specs=[VMEM] * 5,
        out_specs=[VMEM] * 8,
        name="state",
        compiler_params=grant(12 if blocks <= 8 else 24),
    )(taken, arrived, k, v, own)
    scans = [made[:3], made[3:]]

    inside = pl.pallas_call(
        functools.partial(inside_kernel, hd),
        out_shape=shaped((tokens, share), F32),
        in_specs=[VMEM] * 6,
        out_specs=VMEM,
        name="inside",
        compiler_params=grant(12),
    )(q, k, v, c_lanes, c_rows, own)

    bits = [1 << i for i in range(blocks.bit_length() - 1)]
    for bit in bits:
        for g in range(2):
            came = flip(scans[g][0], "seq", bit)
            if bit == bits[-1]:
                scans[g] = [came, *scans[g][1:]]
                continue
            scans[g] = pl.pallas_call(
                functools.partial(step_kernel, bit, hd, bit == 1),
                out_shape=(sent, held, rate, held, rate),
                in_specs=[VMEM] * len(scans[g]),
                out_specs=[VMEM] * 5,
                compiler_params=grant(6 if blocks <= 8 else 24),
            )(came, *scans[g][1:])

    split = tokens * SPLIT // 16
    sizes = (split, tokens - split)
    scratch = [
        pltpu.VMEM((tokens, half * share), BF16),
        pltpu.VMEM((half * share, share), BF16),
    ]
    earlier, carried = pl.pallas_call(
        functools.partial(outside_kernel, bits[-1], range(half), hd),
        out_shape=(shaped((tokens, share), F32), shaped((hd, share), F32)),
        in_specs=[VMEM] * 7,
        out_specs=[VMEM] * 2,
        scratch_shapes=scratch,
        name="outside0",
        compiler_params=grant(8 if blocks <= 8 else 40),
    )(*scans[0], q, own)
    flat, *flats = pl.pallas_call(
        functools.partial(outside_kernel, bits[-1], range(half, blocks), hd),
        out_shape=tuple(shaped((rows, share), BF16) for rows in (tokens,) + sizes),
        in_specs=[VMEM] * 12,
        out_specs=[VMEM] * 3,
        scratch_shapes=scratch,
        name="outside1",
        compiler_params=grant(8 if blocks <= 8 else 40),
    )(*scans[1], q, own, carried, earlier, c_lanes, inside, head_gain.reshape(1, share))

    fetched = pl.pallas_call(
        fetch_kernel,
        out_shape=(
            pltpu.VMEM((tokens, width), BF16),
            pltpu.VMEM(w_out.shape, BF16),
            pltpu.VMEM(w_up.shape, BF16),
            pltpu.VMEM(w_down.shape, BF16),
            pltpu.VMEM((1, width), F32),
        ),
        in_specs=[HBM] * 5,
        out_specs=[VMEM] * 5,
        scratch_shapes=[pltpu.VMEM((width,), BF16), pltpu.SemaphoreType.DMA((5,))],
        name="fetch",
        compiler_params=grant(2),
    )(in_hbm(joined), in_hbm(w_out), w_up, w_down, in_hbm(ffn_gain))

    near_flat = flip(flat, "ffn", 1)
    parts = [gather_flips(part, "ffn") for part in flats]
    hidden = pl.pallas_call(
        own_kernel,
        out_shape=pltpu.VMEM((tokens, width), F32),
        in_specs=[VMEM] * 5,
        out_specs=VMEM,
        name="own",
        compiler_params=grant(6),
    )(flat, near_flat, fetched[1], wout_parts[1], fetched[0])
    finals = []
    for i, rows in enumerate(sizes):
        kept, even, odd = pl.pallas_call(
            functools.partial(ffn_kernel, groups, i * split),
            out_shape=(
                shaped((rows, cols), F32),
                shaped((rows, max(groups // 2 - 1, 1) * cols), F32),
                shaped((rows, groups // 2 * cols), BF16),
            ),
            in_specs=[VMEM] * (2 * groups),
            out_specs=[VMEM] * 3,
            scratch_shapes=[pltpu.VMEM((rows, width), F32)],
            compiler_params=grant(10),
        )(*parts[i][2:], *wout_parts[2:], hidden, fetched[4], *fetched[2:4])
        near = flip(odd, "ffn", 1)
        pieces = {
            j: (
                even[:, (j // 2 - 1) * cols : j // 2 * cols]
                + near[:, j // 2 * cols : (j // 2 + 1) * cols].astype(F32)
            )
            for j in range(2, groups, 2)
        }
        far = [flip(pieces[j].astype(BF16), "ffn", j) for j in pieces]
        far = far[0] if len(far) == 1 else sum(part.astype(F32) for part in far)
        finals += [kept, near, far]
    return pl.pallas_call(
        final_kernel,
        out_shape=shaped((tokens, cols), BF16),
        in_specs=[VMEM] * 6,
        out_specs=VMEM,
        name="final",
        compiler_params=grant(8),
    )(*finals)


def solution(mesh):
    in_specs = (
        P("seq", None),
        P("seq", None),
        P("seq"),
        P("seq", None),
        P("ffn", "seq"),
        P(),
        P(None, "ffn"),
        P(None, "ffn"),
        P(None, "ffn"),
        P("ffn"),
        P("ffn", None),
        P(),
        P(None, "ffn"),
        P("ffn", None),
    )

    return jax.shard_map(
        on_device, mesh=mesh, in_specs=in_specs, out_specs=P("seq", "ffn"), check_vma=False
    )
```

profile of v0, /device:TPU:0, one launch (start us, length us, event | category | flops | bytes accessed | tf_op | source)
XLA Modules:
  0.0 69.8 jit_solution(11153405128876589434)
XLA Ops:
  0.0 3.0 %collective-permute-start.8 = (bf16[256,1024]{1,0:T(8,128)(2,1)}, bf16[256,1024]{1,0:T(8,128)(2,1)S(1)}, u32[]{:S(2)}, u32[]{:S(2)}) collective-permute-start(bf16[256,1024]{1,0:T(8,128)(2,1)} %refs_1_.1), channel_id=1, source_target_pairs={{0,2},{1,3},{2,0},{3,1},{4,6},{5,7},{6,4},{7,5},{8,10},{9,11},{10,... | collective-permute-start | bytes 1572872 | tf_op jit(solution)/shard_map/ppermute | solution.py:344
  3.0 5.8 %all-to-all-start = ((f32[8,4,128]{2,1,0:T(4,128)}), f32[8,4,128]{2,1,0:T(4,128)S(1)}, u32[]{:S(2)}, u32[]{:S(2)}) async-start(f32[8,4,128]{2,1,0:T(4,128)} %bitcast.5), calls=%async_computation | async-start | bytes 32768 | tf_op jit(solution)/shard_map/all_to_all | solution.py:371
  8.8 4.2 %pre.1 = (bf16[512,1024]{1,0:T(8,128)(2,1)}, bf16[512,256]{1,0:T(8,128)(2,1)S(1)}, bf16[512,256]{1,0:T(8,128)(2,1)S(1)}, bf16[512,256]{1,0:T(8,128)(2,1)S(1)}, b...) custom-call(bf16[512,1024]{1,0:T(8,128)(2,1)} %cf.1, bf16[64,1024]{1,0:T(8,128)(2,1)} %pf.1, s32[1,512]{1,0:T(1,128)} %bitcast.6, ...), custom_call_target="tpu_custom_call" | custom-call | tf_op jit(solution)/shard_map/pre/pallas_call | solution.py:408
  13.0 0.0 copy-start
  13.0 0.0 copy-start.1
  13.1 2.3 %all-to-all-done.gates = f32[8,4,128]{2,1,0:T(4,128)S(1)} async-done(((f32[8,4,128]{2,1,0:T(4,128)}), f32[8,4,128]{2,1,0:T(4,128)S(1)}, u32[]{:S(2)}, u32[]{:S(2)}) %all-to-all-start) | async-done | bytes 16416 | tf_op jit(solution)/shard_map/all_to_all | solution.py:371
  15.4 2.2 %state.1 = (f32[512,256]{1,0:T(8,128)S(1)}, f32[8,512]{1,0:T(8,128)S(1)}, bf16[272,256]{1,0:T(8,128)(2,1)S(1)}, f32[4,64,256]{2,1,0:T(8,128)S(1)}, f32[8,256]{1,...) custom-call(bf16[512,1024]{1,0:T(8,128)(2,1)S(1)} %get-tuple-element.55.taken, ...), custom_call_target="tpu_custom_call" | custom-call | tf_op jit(solution)/shard_map/state/pallas_call | solution.py:449
  17.5 0.6 collective-permute-start.3
  18.1 1.5 %collective-permute-start = (bf16[272,256]{1,0:T(8,128)(2,1)S(1)}, bf16[272,256]{1,0:T(8,128)(2,1)S(1)}, u32[]{:S(2)}, u32[]{:S(2)}) collective-permute-start(bf16[272,256]{1,0:T(8,128)(2,1)S(1)} %get-tuple-element.59), channel_id=1, source_target_pairs={{0,4},{4,0},{8,12},{12,8},{16,20},{20,16},{24,28},{28,24},{1,5},{5... | collective-permute-start | bytes 417800 | tf_op jit(solution)/shard_map/ppermute | solution.py:344
  19.6 3.2 %collective-permute-done.3.refs_0_ = bf16[272,256]{1,0:T(8,128)(2,1)S(1)} collective-permute-done((bf16[272,256]{1,0:T(8,128)(2,1)S(1)}, bf16[272,256]{1,0:T(8,128)(2,1)S(1)}, u32[]{:S(2)}, u32[]{:S(2)}) %collective-permute-start.3) | collective-permute-done | bytes 139296 | tf_op jit(solution)/shard_map/ppermute | solution.py:344
  22.8 0.1 shard_map.138
  22.9 0.6 collective-permute-start.4
  23.5 0.8 %collective-permute-done.refs_0_ = bf16[272,256]{1,0:T(8,128)(2,1)S(1)} collective-permute-done((bf16[272,256]{1,0:T(8,128)(2,1)S(1)}, bf16[272,256]{1,0:T(8,128)(2,1)S(1)}, u32[]{:S(2)}, u32[]{:S(2)}) %collective-permute-start) | collective-permute-done | bytes 139296 | tf_op jit(solution)/shard_map/ppermute | solution.py:344
  24.3 0.1 shard_map.136
  24.4 0.7 %collective-permute-start.1 = (bf16[272,256]{1,0:T(8,128)(2,1)S(1)}, bf16[272,256]{1,0:T(8,128)(2,1)S(1)}, u32[]{:S(2)}, u32[]{:S(2)}) collective-permute-start(bf16[272,256]{1,0:T(8,128)(2,1)S(1)} %get-tuple-element.62), channel_id=1, source_target_pairs={{0,8},{4,12},{8,0},{12,4},{16,24},{20,28},{24,16},{28,20},{1,9},{5... | collective-permute-start | bytes 417800 | tf_op jit(solution)/shard_map/ppermute | solution.py:344
  25.1 3.3 %collective-permute-done.4.refs_0_ = bf16[272,256]{1,0:T(8,128)(2,1)S(1)} collective-permute-done((bf16[272,256]{1,0:T(8,128)(2,1)S(1)}, bf16[272,256]{1,0:T(8,128)(2,1)S(1)}, u32[]{:S(2)}, u32[]{:S(2)}) %collective-permute-start.4) | collective-permute-done | bytes 139296 | tf_op jit(solution)/shard_map/ppermute | solution.py:344
  28.4 0.1 shard_map.139
  28.5 2.6 %collective-permute-start.5 = (bf16[272,256]{1,0:T(8,128)(2,1)S(1)}, bf16[272,256]{1,0:T(8,128)(2,1)S(1)}, u32[]{:S(2)}, u32[]{:S(2)}) collective-permute-start(bf16[272,256]{1,0:T(8,128)(2,1)S(1)} %get-tuple-element.81), channel_id=1, source_target_pairs={{0,16},{4,20},{8,24},{12,28},{16,0},{20,4},{24,8},{28,12},{1,17},{... | collective-permute-start | bytes 417800 | tf_op jit(solution)/shard_map/ppermute | solution.py:344
  31.1 0.3 collective-permute-done.1.refs_0_
  31.4 0.1 shard_map.137
  31.5 2.6 %collective-permute-start.2 = (bf16[272,256]{1,0:T(8,128)(2,1)S(1)}, bf16[272,256]{1,0:T(8,128)(2,1)S(1)}, u32[]{:S(2)}, u32[]{:S(2)}) collective-permute-start(bf16[272,256]{1,0:T(8,128)(2,1)S(1)} %get-tuple-element.67), channel_id=1, source_target_pairs={{0,16},{4,20},{8,24},{12,28},{16,0},{20,4},{24,8},{28,12},{1,17},{... | collective-permute-start | bytes 417800 | tf_op jit(solution)/shard_map/ppermute | solution.py:344
  34.1 0.0 collective-permute-start.11
  34.1 0.0 collective-permute-done.8.refs_2_
  34.1 0.5 collective-permute-start.9
  34.6 1.7 %inside.1.refs_10_ = f32[512,256]{1,0:T(8,128)S(1)} custom-call(bf16[512,256]{1,0:T(8,128)(2,1)S(1)} %get-tuple-element.72.refs_5_.q, bf16[512,256]{1,0:T(8,128)(2,1)S(1)} %get-tuple-element.56.k, bf16[512,256]{1,0:T(8,128)(2,1)S(1)} %get-tuple-element.57.v, f32[512,256]{1,0:T(8,128)S(1)} %get-tuple-element.88.c_lanes.refs_9_, ...), custom_call_target="tpu_custom_call" | custom-call | tf_op jit(solution)/shard_map/inside/pallas_call | solution.py:459
  36.3 1.8 %collective-permute-done.5.refs_0_ = bf16[272,256]{1,0:T(8,128)(2,1)S(1)} collective-permute-done((bf16[272,256]{1,0:T(8,128)(2,1)S(1)}, bf16[272,256]{1,0:T(8,128)(2,1)S(1)}, u32[]{:S(2)}, u32[]{:S(2)}) %collective-permute-start.5) | collective-permute-done | bytes 139296 | tf_op jit(solution)/shard_map/ppermute | solution.py:344
  38.1 0.6 outside0.1
  38.7 0.9 %collective-permute-done.2.refs_0_ = bf16[272,256]{1,0:T(8,128)(2,1)S(1)} collective-permute-done((bf16[272,256]{1,0:T(8,128)(2,1)S(1)}, bf16[272,256]{1,0:T(8,128)(2,1)S(1)}, u32[]{:S(2)}, u32[]{:S(2)}) %collective-permute-start.2) | collective-permute-done | bytes 139296 | tf_op jit(solution)/shard_map/ppermute | solution.py:344
  39.6 1.4 %outside1.1 = (bf16[512,256]{1,0:T(8,128)(2,1)S(1)}, bf16[384,256]{1,0:T(8,128)(2,1)S(1)}, bf16[128,256]{1,0:T(8,128)(2,1)S(1)}) custom-call(bf16[272,256]{1,0:T(8,128)(2,1)S(1)} %collective-permute-done.2.refs_0_, f32[4,64,256]{2,1,0:T(8,128)S(1)} %get-tuple-element.68.refs_1_, f32[8,256]{1,0:T(8,128)S(1)} %get-tuple-element.69.refs_2_, ...), custom_call_target="tpu_custom_call" | custom-call | tf_op jit(solution)/shard_map/outside1/pallas_call | solution.py:498
  40.9 0.6 collective-permute-start.6
  41.5 5.1 %collective-permute-done.6.refs_0_ = bf16[384,256]{1,0:T(8,128)(2,1)S(1)} collective-permute-done((bf16[384,256]{1,0:T(8,128)(2,1)S(1)}, bf16[384,256]{1,0:T(8,128)(2,1)S(1)}, u32[]{:S(2)}, u32[]{:S(2)}) %collective-permute-start.6) | collective-permute-done | bytes 196640 | tf_op jit(solution)/shard_map/ppermute | solution.py:344
  46.7 0.0 collective-permute-start.7
  46.7 2.8 %fetch.1 = (bf16[512,1024]{1,0:T(8,128)(2,1)S(1)}, bf16[256,1024]{1,0:T(8,128)(2,1)S(1)}, bf16[1024,1024]{1,0:T(8,128)(2,1)S(1)}, bf16[1024,1024]{1,0:T(8,128)(2,1)S(1)}, f32[1,1024]{1,0:T(1,128)S(1)}) custom-call(bf16[512,1024]{1,0:T(8,128)(2,1)} %get-tuple-element.92.refs_0_, bf16[256,1024]{1,0:T(8,128)(2,1)} %refs_1_.1, bf16[1024,1024]{1,0:T(8,128)(2,1)} %refs_2_.1, ...), custom_call_target="tpu_custom_call" | custom-call | tf_op jit(solution)/shard_map/fetch/pallas_call | solution.py:508
  49.5 0.0 collective-permute-done.10.near
  49.5 0.7 %own.1.refs_4_ = f32[512,1024]{1,0:T(8,128)S(1)} custom-call(bf16[512,256]{1,0:T(8,128)(2,1)S(1)} %get-tuple-element.91.mine, bf16[512,256]{1,0:T(8,128)(2,1)S(1)} %collective-permute-done.10.near, bf16[256,1024]{1,0:T(8,128)(2,1)S(1)} %get-tuple-element.93.own_w, bf16[256,1024]{1,0:T(8,128)(2,1)S(1)} %collective-permute-done.11.near_w, ...), custom_call_target="tpu_custom_call" | custom-call | tf_op jit(solution)/shard_map/own/pallas_call | solution.py:526
  50.2 0.0 collective-permute-done.7.refs_1_
  50.2 2.5 %shard_map.140 = (f32[384,256]{1,0:T(8,128)S(1)}, f32[384,256]{1,0:T(8,128)S(1)}, bf16[384,512]{1,0:T(8,128)(2,1)S(1)}) custom-call(bf16[384,256]{1,0:T(8,128)(2,1)S(1)} %collective-permute-done.6.refs_0_, bf16[384,256]{1,0:T(8,128)(2,1)S(1)} %collective-permute-done.7.refs_1_, bf16[256,1024]{1,0:T(8,128)(2,1)S(1)} %collective-permute-done.8.refs_2_, ...), custom_call_target="tpu_custom_call" | custom-call | tf_op jit(solution)/shard_map/pallas_call | solution.py:536
  52.7 0.6 collective-permute-start.12
  53.3 0.5 collective-permute-start.14
  53.9 3.7 %collective-permute-done.14.refs_0_ = bf16[128,256]{1,0:T(8,128)(2,1)S(1)} collective-permute-done((bf16[128,256]{1,0:T(8,128)(2,1)S(1)}, bf16[128,256]{1,0:T(8,128)(2,1)S(1)}, u32[]{:S(2)}, u32[]{:S(2)}) %collective-permute-start.14) | collective-permute-done | bytes 65568 | tf_op jit(solution)/shard_map/ppermute | solution.py:344
  57.6 1.3 %collective-permute-done.15.refs_1_ = bf16[128,256]{1,0:T(8,128)(2,1)S(1)} collective-permute-done((bf16[128,256]{1,0:T(8,128)(2,1)S(1)}, bf16[128,256]{1,0:T(8,128)(2,1)S(1)}, u32[]{:S(2)}, u32[]{:S(2)}) %collective-permute-start.15) | collective-permute-done | bytes 65568 | tf_op jit(solution)/shard_map/ppermute | solution.py:344
  58.8 1.2 %shard_map.141 = (f32[128,256]{1,0:T(8,128)S(1)}, f32[128,256]{1,0:T(8,128)S(1)}, bf16[128,512]{1,0:T(8,128)(2,1)S(1)}) custom-call(bf16[128,256]{1,0:T(8,128)(2,1)S(1)} %collective-permute-done.14.refs_0_, bf16[128,256]{1,0:T(8,128)(2,1)S(1)} %collective-permute-done.15.refs_1_, bf16[256,1024]{1,0:T(8,128)(2,1)S(1)} %collective-permute-done.8.refs_2_, ...), custom_call_target="tpu_custom_call" | custom-call | tf_op jit(solution)/shard_map/pallas_call | solution.py:536
  60.1 0.2 collective-permute-start.16
  60.3 0.6 collective-permute-start.13
  60.9 0.5 collective-permute-done.16.refs_4_
  61.5 1.0 %collective-permute-start.17 = (bf16[128,256]{1,0:T(8,128)(2,1)S(1)}, bf16[128,256]{1,0:T(8,128)(2,1)S(1)}, u32[]{:S(2)}, u32[]{:S(2)}) collective-permute-start(bf16[128,256]{1,0:T(8,128)(2,1)S(1)} %add_convert_fusion.1), channel_id=1, source_target_pairs={{0,2},{1,3},{2,0},{3,1},{4,6},{5,7},{6,4},{7,5},{8,10},{9,11},{10,... | collective-permute-start | bytes 196616 | tf_op jit(solution)/shard_map/ppermute | solution.py:344
  62.5 6.5 %collective-permute-done.17.refs_5_ = bf16[128,256]{1,0:T(8,128)(2,1)S(1)} collective-permute-done((bf16[128,256]{1,0:T(8,128)(2,1)S(1)}, bf16[128,256]{1,0:T(8,128)(2,1)S(1)}, u32[]{:S(2)}, u32[]{:S(2)}) %collective-permute-start.17) | collective-permute-done | bytes 65568 | tf_op jit(solution)/shard_map/ppermute | solution.py:344
  69.0 0.8 %final.1 = bf16[512,256]{1,0:T(8,128)(2,1)} custom-call(f32[384,256]{1,0:T(8,128)S(1)} %get-tuple-element.98.refs_0_, bf16[384,512]{1,0:T(8,128)(2,1)S(1)} %collective-permute-done.12.refs_1_, bf16[384,256]{1,0:T(8,128)(2,1)S(1)} %collective-permute-done.13.refs_2_, f32[128,256]{1,0:T(8,128)S(1)} %get-tuple-element.102.refs_3_, ...), custom_call_target="tpu_custom_call" | custom-call | tf_op jit(solution)/shard_map/final/pallas_call | solution.py:559
  (11 shorter events, 0.1 us)
Async XLA Ops:
  0.0 34.1 %collective-permute-start.8 = (bf16[256,1024]{1,0:T(8,128)(2,1)}, bf16[256,1024]{1,0:T(8,128)(2,1)S(1)}, u32[]{:S(2)}, u32[]{:S(2)}) collective-permute-start(bf16[256,1024]{1,0:T(8,128)(2,1)} %refs_1_.1), channel_id=1, source_target_pairs={{0,2},{1,3},{2,0},{3,1},{4,6},{5,7},{6,4},{7,5},{8,10},{9,11},{10,... | collective-permute-start | bytes 1572872 | tf_op jit(solution)/shard_map/ppermute | solution.py:344
  3.0 12.4 %all-to-all-start = ((f32[8,4,128]{2,1,0:T(4,128)}), f32[8,4,128]{2,1,0:T(4,128)S(1)}, u32[]{:S(2)}, u32[]{:S(2)}) async-start(f32[8,4,128]{2,1,0:T(4,128)} %bitcast.5), calls=%async_computation | async-start | bytes 32768 | tf_op jit(solution)/shard_map/all_to_all | solution.py:371
  13.0 21.1 %copy-start = (bf16[256,1024]{1,0:T(8,128)(2,1)S(1)}, bf16[256,1024]{1,0:T(8,128)(2,1)}, u32[]{:S(2)}) copy-start(bf16[256,1024]{1,0:T(8,128)(2,1)} %refs_1_.1) | copy-start | bytes 1572868
  13.0 21.6 %copy-start.1 = (bf16[256]{0:T(256)(128)(2,1)S(1)}, bf16[256]{0:T(256)(128)(2,1)}, u32[]{:S(2)}) copy-start(bf16[256]{0:T(256)(128)(2,1)} %param.23) | copy-start | bytes 1540
  17.5 5.3 %collective-permute-start.3 = (bf16[272,256]{1,0:T(8,128)(2,1)S(1)}, bf16[272,256]{1,0:T(8,128)(2,1)S(1)}, u32[]{:S(2)}, u32[]{:S(2)}) collective-permute-start(bf16[272,256]{1,0:T(8,128)(2,1)S(1)} %get-tuple-element.73), channel_id=1, source_target_pairs={{0,4},{4,0},{8,12},{12,8},{16,20},{20,16},{24,28},{28,24},{1,5},{5... | collective-permute-start | bytes 417800 | tf_op jit(solution)/shard_map/ppermute | solution.py:344
  18.1 6.2 %collective-permute-start = (bf16[272,256]{1,0:T(8,128)(2,1)S(1)}, bf16[272,256]{1,0:T(8,128)(2,1)S(1)}, u32[]{:S(2)}, u32[]{:S(2)}) collective-permute-start(bf16[272,256]{1,0:T(8,128)(2,1)S(1)} %get-tuple-element.59), channel_id=1, source_target_pairs={{0,4},{4,0},{8,12},{12,8},{16,20},{20,16},{24,28},{28,24},{1,5},{5... | collective-permute-start | bytes 417800 | tf_op jit(solution)/shard_map/ppermute | solution.py:344
  22.9 5.6 %collective-permute-start.4 = (bf16[272,256]{1,0:T(8,128)(2,1)S(1)}, bf16[272,256]{1,0:T(8,128)(2,1)S(1)}, u32[]{:S(2)}, u32[]{:S(2)}) collective-permute-start(bf16[272,256]{1,0:T(8,128)(2,1)S(1)} %get-tuple-element.76), channel_id=1, source_target_pairs={{0,8},{4,12},{8,0},{12,4},{16,24},{20,28},{24,16},{28,20},{1,9},{5... | collective-permute-start | bytes 417800 | tf_op jit(solution)/shard_map/ppermute | solution.py:344
  24.4 7.1 %collective-permute-start.1 = (bf16[272,256]{1,0:T(8,128)(2,1)S(1)}, bf16[272,256]{1,0:T(8,128)(2,1)S(1)}, u32[]{:S(2)}, u32[]{:S(2)}) collective-permute-start(bf16[272,256]{1,0:T(8,128)(2,1)S(1)} %get-tuple-element.62), channel_id=1, source_target_pairs={{0,8},{4,12},{8,0},{12,4},{16,24},{20,28},{24,16},{28,20},{1,9},{5... | collective-permute-start | bytes 417800 | tf_op jit(solution)/shard_map/ppermute | solution.py:344
  28.5 9.5 %collective-permute-start.5 = (bf16[272,256]{1,0:T(8,128)(2,1)S(1)}, bf16[272,256]{1,0:T(8,128)(2,1)S(1)}, u32[]{:S(2)}, u32[]{:S(2)}) collective-permute-start(bf16[272,256]{1,0:T(8,128)(2,1)S(1)} %get-tuple-element.81), channel_id=1, source_target_pairs={{0,16},{4,20},{8,24},{12,28},{16,0},{20,4},{24,8},{28,12},{1,17},{... | collective-permute-start | bytes 417800 | tf_op jit(solution)/shard_map/ppermute | solution.py:344
  31.5 8.0 %collective-permute-start.2 = (bf16[272,256]{1,0:T(8,128)(2,1)S(1)}, bf16[272,256]{1,0:T(8,128)(2,1)S(1)}, u32[]{:S(2)}, u32[]{:S(2)}) collective-permute-start(bf16[272,256]{1,0:T(8,128)(2,1)S(1)} %get-tuple-element.67), channel_id=1, source_target_pairs={{0,16},{4,20},{8,24},{12,28},{16,0},{20,4},{24,8},{28,12},{1,17},{... | collective-permute-start | bytes 417800 | tf_op jit(solution)/shard_map/ppermute | solution.py:344
  34.1 15.4 %collective-permute-start.11 = (bf16[256,1024]{1,0:T(8,128)(2,1)S(1)}, bf16[256,1024]{1,0:T(8,128)(2,1)S(1)}, u32[]{:S(2)}, u32[]{:S(2)}) collective-permute-start(bf16[256,1024]{1,0:T(8,128)(2,1)S(1)} %copy-done), channel_id=1, source_target_pairs={{0,1},{1,0},{2,3},{3,2},{4,5},{5,4},{6,7},{7,6},{8,9},{9,8},{10,11... | collective-permute-start | bytes 1572872 | tf_op jit(solution)/shard_map/ppermute | solution.py:344
  34.1 16.1 %collective-permute-start.9 = (bf16[256,1024]{1,0:T(8,128)(2,1)S(1)}, bf16[256,1024]{1,0:T(8,128)(2,1)S(1)}, u32[]{:S(2)}, u32[]{:S(2)}) collective-permute-start(bf16[256,1024]{1,0:T(8,128)(2,1)S(1)} %collective-permute-done.8.refs_2_), channel_id=1, source_target_pairs={{0,1},{1,0},{2,3},{3,2},{4,5},{5,4},{6,7},{7,6},{8,9},{9,8},{10,11... | collective-permute-start | bytes 1572872 | tf_op jit(solution)/shard_map/ppermute | solution.py:344
  40.9 5.7 %collective-permute-start.6 = (bf16[384,256]{1,0:T(8,128)(2,1)S(1)}, bf16[384,256]{1,0:T(8,128)(2,1)S(1)}, u32[]{:S(2)}, u32[]{:S(2)}) collective-permute-start(bf16[384,256]{1,0:T(8,128)(2,1)S(1)} %get-tuple-element.90), channel_id=1, source_target_pairs={{0,2},{1,3},{2,0},{3,1},{4,6},{5,7},{6,4},{7,5},{8,10},{9,11},{10,... | collective-permute-start | bytes 589832 | tf_op jit(solution)/shard_map/ppermute | solution.py:344
  41.5 7.9 %collective-permute-start.10 = (bf16[512,256]{1,0:T(8,128)(2,1)S(1)}, bf16[512,256]{1,0:T(8,128)(2,1)S(1)}, u32[]{:S(2)}, u32[]{:S(2)}) collective-permute-start(bf16[512,256]{1,0:T(8,128)(2,1)S(1)} %get-tuple-element.91.mine), channel_id=1, source_target_pairs={{0,1},{1,0},{2,3},{3,2},{4,5},{5,4},{6,7},{7,6},{8,9},{9,8},{10,11... | collective-permute-start | bytes 786440 | tf_op jit(solution)/shard_map/ppermute | solution.py:344
  46.7 3.5 %collective-permute-start.7 = (bf16[384,256]{1,0:T(8,128)(2,1)S(1)}, bf16[384,256]{1,0:T(8,128)(2,1)S(1)}, u32[]{:S(2)}, u32[]{:S(2)}) collective-permute-start(bf16[384,256]{1,0:T(8,128)(2,1)S(1)} %collective-permute-done.6.refs_0_), channel_id=1, source_target_pairs={{0,1},{1,0},{2,3},{3,2},{4,5},{5,4},{6,7},{7,6},{8,9},{9,8},{10,11... | collective-permute-start | bytes 589832 | tf_op jit(solution)/shard_map/ppermute | solution.py:344
  52.7 7.5 %collective-permute-start.12 = (bf16[384,512]{1,0:T(8,128)(2,1)S(1)}, bf16[384,512]{1,0:T(8,128)(2,1)S(1)}, u32[]{:S(2)}, u32[]{:S(2)}) collective-permute-start(bf16[384,512]{1,0:T(8,128)(2,1)S(1)} %get-tuple-element.99), channel_id=1, source_target_pairs={{0,1},{1,0},{2,3},{3,2},{4,5},{5,4},{6,7},{7,6},{8,9},{9,8},{10,11... | collective-permute-start | bytes 1179656 | tf_op jit(solution)/shard_map/ppermute | solution.py:344
  53.3 4.3 %collective-permute-start.14 = (bf16[128,256]{1,0:T(8,128)(2,1)S(1)}, bf16[128,256]{1,0:T(8,128)(2,1)S(1)}, u32[]{:S(2)}, u32[]{:S(2)}) collective-permute-start(bf16[128,256]{1,0:T(8,128)(2,1)S(1)} %get-tuple-element.101), channel_id=1, source_target_pairs={{0,2},{1,3},{2,0},{3,1},{4,6},{5,7},{6,4},{7,5},{8,10},{9,11},{10,... | collective-permute-start | bytes 196616 | tf_op jit(solution)/shard_map/ppermute | solution.py:344
  57.6 1.3 %collective-permute-start.15 = (bf16[128,256]{1,0:T(8,128)(2,1)S(1)}, bf16[128,256]{1,0:T(8,128)(2,1)S(1)}, u32[]{:S(2)}, u32[]{:S(2)}) collective-permute-start(bf16[128,256]{1,0:T(8,128)(2,1)S(1)} %collective-permute-done.14.refs_0_), channel_id=1, source_target_pairs={{0,1},{1,0},{2,3},{3,2},{4,5},{5,4},{6,7},{7,6},{8,9},{9,8},{10,11... | collective-permute-start | bytes 196616 | tf_op jit(solution)/shard_map/ppermute | solution.py:344
  60.1 1.4 %collective-permute-start.16 = (bf16[128,512]{1,0:T(8,128)(2,1)S(1)}, bf16[128,512]{1,0:T(8,128)(2,1)S(1)}, u32[]{:S(2)}, u32[]{:S(2)}) collective-permute-start(bf16[128,512]{1,0:T(8,128)(2,1)S(1)} %get-tuple-element.103), channel_id=1, source_target_pairs={{0,1},{1,0},{2,3},{3,2},{4,5},{5,4},{6,7},{7,6},{8,9},{9,8},{10,11... | collective-permute-start | bytes 393224 | tf_op jit(solution)/shard_map/ppermute | solution.py:344
  60.3 8.6 %collective-permute-start.13 = (bf16[384,256]{1,0:T(8,128)(2,1)S(1)}, bf16[384,256]{1,0:T(8,128)(2,1)S(1)}, u32[]{:S(2)}, u32[]{:S(2)}) collective-permute-start(bf16[384,256]{1,0:T(8,128)(2,1)S(1)} %add_convert_fusion), channel_id=1, source_target_pairs={{0,2},{1,3},{2,0},{3,1},{4,6},{5,7},{6,4},{7,5},{8,10},{9,11},{10,... | collective-permute-start | bytes 589832 | tf_op jit(solution)/shard_map/ppermute | solution.py:344
  61.5 7.5 %collective-permute-start.17 = (bf16[128,256]{1,0:T(8,128)(2,1)S(1)}, bf16[128,256]{1,0:T(8,128)(2,1)S(1)}, u32[]{:S(2)}, u32[]{:S(2)}) collective-permute-start(bf16[128,256]{1,0:T(8,128)(2,1)S(1)} %add_convert_fusion.1), channel_id=1, source_target_pairs={{0,2},{1,3},{2,0},{3,1},{4,6},{5,7},{6,4},{7,5},{8,10},{9,11},{10,... | collective-permute-start | bytes 196616 | tf_op jit(solution)/shard_map/ppermute | solution.py:344
where the time goes:
time: 70 us; the launch traced here: 69.8 us
  waiting for transfers between devices  29.7 us (42%)
  starting transfers between devices  21.5 us (31%)
  Pallas kernels  18.3 us (26%)
    ppermute x18, waiting for transfers between devices, flip(): return lax.ppermute(array, axis, [(i, i ^ bit) for i in range(size)])  27.3 us
    ppermute x18, starting transfers between devices, flip(): return lax.ppermute(array, axis, [(i, i ^ bit) for i in range(size)])  15.7 us
    all_to_all x1, starting transfers between devices, exchange(): return lax.all_to_all(array, 'seq', split_axis=0, concat_axis=0, tiled=True)  5.83 us
    pallas_call x1, Pallas kernels, on_device(): pl.pallas_call(functools.partial(pre_kernel, cap, blocks), out_shape=(plt...  4.22 us
    pallas_call x2, Pallas kernels, on_device(): pl.pallas_call(functools.partial(ffn_kernel, groups, i * split), out_shap...  3.73 us
    pallas_call x1, Pallas kernels, on_device(): pl.pallas_call(fetch_kernel, out_shape=(pltpu.VMEM((tokens, width), BF16)...  2.77 us
    all_to_all x1, waiting for transfers between devices, exchange(): return lax.all_to_all(array, 'seq', split_axis=0, concat_axis=0, tiled=True)  2.32 us
    pallas_call x1, Pallas kernels, on_device(): pl.pallas_call(functools.partial(state_kernel, cap, blocks, hd), out_shap...  2.15 us
  transfers between devices with their start and end apart: 19, of which 12 were waited for; matrix products, arithmetic and copies ran while one was open for 0% of the time, Pallas kernels for 21%

commit v1 on v0

--- a/solution.py
+++ b/solution.py
@@ -57,7 +57,7 @@
 def pre_kernel(
     cap, blocks, cf, pf, pick, own, gain, wq, wk, wv,
     joined, q, k, v, taken, own_out,
-    cf_v, pf_v, pick_v, own_v, gain_v, w_v, joined_v, sems, out_sems,
+    cf_v, pf_v, pick_v, own_v, gain_v, w_v, sems,
 ):
     tokens = cf.shape[0]
     parents = pf.shape[0]
@@ -87,25 +87,19 @@
     for copy in small[1:4]:
         copy.wait()
     scales = gain_v[...].astype(F32).reshape(1, -1)
-    stores = []
     for i, at in enumerate(starts):
         rows = pl.ds(at, tile)
         parts[i].wait()
         chosen = jnp.where(iota((parents, tile), 0) == pick_v[:, rows], 1.0, 0.0).astype(BF16)
         added = lax.dot_general(chosen, pf_v[...], TN, preferred_element_type=F32)
         summed = (cf_v[rows, :].astype(F32) + added).astype(BF16)
-        joined_v[rows, :] = summed
-        store = pltpu.make_async_copy(joined_v.at[rows], joined.at[rows], out_sems.at[i])
-        store.start()
-        stores.append(store)
+        joined[rows, :] = summed
         normed = row_norm(summed.astype(F32), scales).astype(BF16)
         if i == 0:
             for copy in weights:
                 copy.wait()
         for j, out in enumerate((q, k, v)):
             out[rows, :] = dot(normed, w_v[j]).astype(BF16)
-    for store in stores:
-        store.wait()
 
 
 def gate_rows(gates, blocks):
@@ -284,7 +278,7 @@
 
 
 def fetch_kernel(*refs):
-    sources, gain, outs, (scale, gain_v, sems) = refs[:4], refs[4], refs[5:9], refs[9:]
+    sources, gain, outs, (scale, gain_v, sems) = refs[:3], refs[3], refs[4:7], refs[7:]
     copies = fetch([(gain, gain_v), *zip(sources, outs)], sems)
     copies[0].wait()
     scale[...] = gain_v[...].astype(F32).reshape(1, -1)
@@ -408,7 +402,7 @@
     joined, q, k, v, taken, own = pl.pallas_call(
         functools.partial(pre_kernel, cap, blocks),
         out_shape=(
-            pltpu.HBM((tokens, width), BF16),
+            shaped((tokens, width), BF16),
             shaped((tokens, share), BF16),
             shaped((tokens, share), BF16),
             shaped((tokens, share), BF16),
@@ -416,7 +410,7 @@
             shaped((1, tokens), jnp.int32),
         ),
         in_specs=[HBM] * 8,
-        out_specs=[HBM] + [VMEM] * 5,
+        out_specs=[VMEM] * 6,
         scratch_shapes=[
             pltpu.VMEM((tokens, width), BF16),
             pltpu.VMEM(parent_feat.shape, BF16),
@@ -424,9 +418,7 @@
             pltpu.VMEM((1, tokens), jnp.int32),
             pltpu.VMEM((width,), BF16),
             pltpu.VMEM((3, width, share), BF16),
-            pltpu.VMEM((tokens, width), BF16),
             pltpu.SemaphoreType.DMA((7 + tiles,)),
-            pltpu.SemaphoreType.DMA((tiles,)),
         ],
         name="pre",
         compiler_params=grant(20),
@@ -508,18 +500,17 @@
     fetched = pl.pallas_call(
         fetch_kernel,
         out_shape=(
-            pltpu.VMEM((tokens, width), BF16),
             pltpu.VMEM(w_out.shape, BF16),
             pltpu.VMEM(w_up.shape, BF16),
             pltpu.VMEM(w_down.shape, BF16),
             pltpu.VMEM((1, width), F32),
         ),
-        in_specs=[HBM] * 5,
-        out_specs=[VMEM] * 5,
-        scratch_shapes=[pltpu.VMEM((width,), BF16), pltpu.SemaphoreType.DMA((5,))],
+        in_specs=[HBM] * 4,
+        out_specs=[VMEM] * 4,
+        scratch_shapes=[pltpu.VMEM((width,), BF16), pltpu.SemaphoreType.DMA((4,))],
         name="fetch",
         compiler_params=grant(2),
-    )(in_hbm(joined), in_hbm(w_out), w_up, w_down, in_hbm(ffn_gain))
+    )(in_hbm(w_out), w_up, w_down, in_hbm(ffn_gain))
 
     near_flat = flip(flat, "ffn", 1)
     parts = [gather_flips(part, "ffn") for part in flats]
@@ -530,7 +521,7 @@
         out_specs=VMEM,
         name="own",
         compiler_params=grant(6),
-    )(flat, near_flat, fetched[1], wout_parts[1], fetched[0])
+    )(flat, near_flat, fetched[0], wout_parts[1], joined)
     finals = []
     for i, rows in enumerate(sizes):
         kept, even, odd = pl.pallas_call(
@@ -544,7 +535,7 @@
             out_specs=[VMEM] * 3,
             scratch_shapes=[pltpu.VMEM((rows, width), F32)],
             compiler_params=grant(10),
-        )(*parts[i][2:], *wout_parts[2:], hidden, fetched[4], *fetched[2:4])
+        )(*parts[i][2:], *wout_parts[2:], hidden, fetched[3], *fetched[1:3])
         near = flip(odd, "ffn", 1)
         pieces = {
             j: (

time: 70 us -> 69.7 us (level)
  no operation moved by 1% of the time
where the time goes in v1:
time: 69.7 us; the launch traced here: 69.5 us
  waiting for transfers between devices  29.8 us (43%)
  starting transfers between devices  21.5 us (31%)
  Pallas kernels  18 us (26%)
    ppermute x18, waiting for transfers between devices, flip(): return lax.ppermute(array, axis, [(i, i ^ bit) for i in range(size)])  27.4 us
    ppermute x18, starting transfers between devices, flip(): return lax.ppermute(array, axis, [(i, i ^ bit) for i in range(size)])  15.7 us
    all_to_all x1, starting transfers between devices, exchange(): return lax.all_to_all(array, 'seq', split_axis=0, concat_axis=0, tiled=True)  5.83 us
    pallas_call x1, Pallas kernels, on_device(): pl.pallas_call(functools.partial(pre_kernel, cap, blocks), out_shape=(sha...  4.18 us
    pallas_call x2, Pallas kernels, on_device(): pl.pallas_call(functools.partial(ffn_kernel, groups, i * split), out_shap...  3.78 us
    pallas_call x1, Pallas kernels, on_device(): pl.pallas_call(fetch_kernel, out_shape=(pltpu.VMEM(w_out.shape, BF16), pl...  2.45 us
    all_to_all x1, waiting for transfers between devices, exchange(): return lax.all_to_all(array, 'seq', split_axis=0, concat_axis=0, tiled=True)  2.37 us
    pallas_call x1, Pallas kernels, on_device(): pl.pallas_call(functools.partial(state_kernel, cap, blocks, hd), out_shap...  2.16 us
  transfers between devices with their start and end apart: 19, of which 12 were waited for; matrix products, arithmetic and copies ran while one was open for 0% of the time, Pallas kernels for 21%

profile of v1, /device:TPU:0, one launch (start us, length us, event | category | flops | bytes accessed | tf_op | source)
XLA Modules:
  0.0 69.5 jit_solution(13928941759179132167)
XLA Ops:
  0.0 3.0 %collective-permute-start.8 = (bf16[256,1024]{1,0:T(8,128)(2,1)}, bf16[256,1024]{1,0:T(8,128)(2,1)S(1)}, u32[]{:S(2)}, u32[]{:S(2)}) collective-permute-start(bf16[256,1024]{1,0:T(8,128)(2,1)} %refs_0_.1), channel_id=1, source_target_pairs={{0,2},{1,3},{2,0},{3,1},{4,6},{5,7},{6,4},{7,5},{8,10},{9,11},{10,... | collective-permute-start | bytes 1572872 | tf_op jit(solution)/shard_map/ppermute | solution.py:338
  3.0 5.8 %all-to-all-start = ((f32[8,4,128]{2,1,0:T(4,128)}), f32[8,4,128]{2,1,0:T(4,128)S(1)}, u32[]{:S(2)}, u32[]{:S(2)}) async-start(f32[8,4,128]{2,1,0:T(4,128)} %bitcast.5), calls=%async_computation | async-start | bytes 32768 | tf_op jit(solution)/shard_map/all_to_all | solution.py:365
  8.8 4.2 %pre.1 = (bf16[512,1024]{1,0:T(8,128)(2,1)S(1)}, bf16[512,256]{1,0:T(8,128)(2,1)S(1)}, bf16[512,256]{1,0:T(8,128)(2,1)S(1)}, bf16[512,256]{1,0:T(8,128)(2,1)S(1)...) custom-call(bf16[512,1024]{1,0:T(8,128)(2,1)} %cf.1, bf16[64,1024]{1,0:T(8,128)(2,1)} %pf.1, s32[1,512]{1,0:T(1,128)} %bitcast.6, ...), custom_call_target="tpu_custom_call" | custom-call | tf_op jit(solution)/shard_map/pre/pallas_call | solution.py:402
  13.0 0.0 copy-start.1
  13.0 2.4 %all-to-all-done.gates = f32[8,4,128]{2,1,0:T(4,128)S(1)} async-done(((f32[8,4,128]{2,1,0:T(4,128)}), f32[8,4,128]{2,1,0:T(4,128)S(1)}, u32[]{:S(2)}, u32[]{:S(2)}) %all-to-all-start) | async-done | bytes 16416 | tf_op jit(solution)/shard_map/all_to_all | solution.py:365
  15.4 2.2 %state.1 = (f32[512,256]{1,0:T(8,128)S(1)}, f32[8,512]{1,0:T(8,128)S(1)}, bf16[272,256]{1,0:T(8,128)(2,1)S(1)}, f32[4,64,256]{2,1,0:T(8,128)S(1)}, f32[8,256]{1,...) custom-call(bf16[512,1024]{1,0:T(8,128)(2,1)S(1)} %get-tuple-element.54.taken, ...), custom_call_target="tpu_custom_call" | custom-call | tf_op jit(solution)/shard_map/state/pallas_call | solution.py:441
  17.5 0.6 collective-permute-start.3
  18.1 1.5 %collective-permute-start = (bf16[272,256]{1,0:T(8,128)(2,1)S(1)}, bf16[272,256]{1,0:T(8,128)(2,1)S(1)}, u32[]{:S(2)}, u32[]{:S(2)}) collective-permute-start(bf16[272,256]{1,0:T(8,128)(2,1)S(1)} %get-tuple-element.58), channel_id=1, source_target_pairs={{0,4},{4,0},{8,12},{12,8},{16,20},{20,16},{24,28},{28,24},{1,5},{5... | collective-permute-start | bytes 417800 | tf_op jit(solution)/shard_map/ppermute | solution.py:338
  19.6 3.2 %collective-permute-done.3.refs_0_ = bf16[272,256]{1,0:T(8,128)(2,1)S(1)} collective-permute-done((bf16[272,256]{1,0:T(8,128)(2,1)S(1)}, bf16[272,256]{1,0:T(8,128)(2,1)S(1)}, u32[]{:S(2)}, u32[]{:S(2)}) %collective-permute-start.3) | collective-permute-done | bytes 139296 | tf_op jit(solution)/shard_map/ppermute | solution.py:338
  22.8 0.1 shard_map.138
  22.9 0.6 collective-permute-start.4
  23.5 0.8 %collective-permute-done.refs_0_ = bf16[272,256]{1,0:T(8,128)(2,1)S(1)} collective-permute-done((bf16[272,256]{1,0:T(8,128)(2,1)S(1)}, bf16[272,256]{1,0:T(8,128)(2,1)S(1)}, u32[]{:S(2)}, u32[]{:S(2)}) %collective-permute-start) | collective-permute-done | bytes 139296 | tf_op jit(solution)/shard_map/ppermute | solution.py:338
  24.3 0.1 shard_map.136
  24.4 0.7 %collective-permute-start.1 = (bf16[272,256]{1,0:T(8,128)(2,1)S(1)}, bf16[272,256]{1,0:T(8,128)(2,1)S(1)}, u32[]{:S(2)}, u32[]{:S(2)}) collective-permute-start(bf16[272,256]{1,0:T(8,128)(2,1)S(1)} %get-tuple-element.61), channel_id=1, source_target_pairs={{0,8},{4,12},{8,0},{12,4},{16,24},{20,28},{24,16},{28,20},{1,9},{5... | collective-permute-start | bytes 417800 | tf_op jit(solution)/shard_map/ppermute | solution.py:338
  25.1 3.3 %collective-permute-done.4.refs_0_ = bf16[272,256]{1,0:T(8,128)(2,1)S(1)} collective-permute-done((bf16[272,256]{1,0:T(8,128)(2,1)S(1)}, bf16[272,256]{1,0:T(8,128)(2,1)S(1)}, u32[]{:S(2)}, u32[]{:S(2)}) %collective-permute-start.4) | collective-permute-done | bytes 139296 | tf_op jit(solution)/shard_map/ppermute | solution.py:338
  28.4 0.1 shard_map.139
  28.5 2.6 %collective-permute-start.5 = (bf16[272,256]{1,0:T(8,128)(2,1)S(1)}, bf16[272,256]{1,0:T(8,128)(2,1)S(1)}, u32[]{:S(2)}, u32[]{:S(2)}) collective-permute-start(bf16[272,256]{1,0:T(8,128)(2,1)S(1)} %get-tuple-element.80), channel_id=1, source_target_pairs={{0,16},{4,20},{8,24},{12,28},{16,0},{20,4},{24,8},{28,12},{1,17},{... | collective-permute-start | bytes 417800 | tf_op jit(solution)/shard_map/ppermute | solution.py:338
  31.1 0.3 collective-permute-done.1.refs_0_
  31.4 0.1 shard_map.137
  31.5 2.6 %collective-permute-start.2 = (bf16[272,256]{1,0:T(8,128)(2,1)S(1)}, bf16[272,256]{1,0:T(8,128)(2,1)S(1)}, u32[]{:S(2)}, u32[]{:S(2)}) collective-permute-start(bf16[272,256]{1,0:T(8,128)(2,1)S(1)} %get-tuple-element.66), channel_id=1, source_target_pairs={{0,16},{4,20},{8,24},{12,28},{16,0},{20,4},{24,8},{28,12},{1,17},{... | collective-permute-start | bytes 417800 | tf_op jit(solution)/shard_map/ppermute | solution.py:338
  34.1 0.0 collective-permute-start.11
  34.1 0.5 collective-permute-start.9
  34.6 1.6 %inside.1.refs_10_ = f32[512,256]{1,0:T(8,128)S(1)} custom-call(bf16[512,256]{1,0:T(8,128)(2,1)S(1)} %get-tuple-element.71.refs_5_.q, bf16[512,256]{1,0:T(8,128)(2,1)S(1)} %get-tuple-element.55.k, bf16[512,256]{1,0:T(8,128)(2,1)S(1)} %get-tuple-element.56.v, f32[512,256]{1,0:T(8,128)S(1)} %get-tuple-element.87.c_lanes.refs_9_, ...), custom_call_target="tpu_custom_call" | custom-call | tf_op jit(solution)/shard_map/inside/pallas_call | solution.py:451
  36.2 1.9 %collective-permute-done.5.refs_0_ = bf16[272,256]{1,0:T(8,128)(2,1)S(1)} collective-permute-done((bf16[272,256]{1,0:T(8,128)(2,1)S(1)}, bf16[272,256]{1,0:T(8,128)(2,1)S(1)}, u32[]{:S(2)}, u32[]{:S(2)}) %collective-permute-start.5) | collective-permute-done | bytes 139296 | tf_op jit(solution)/shard_map/ppermute | solution.py:338
  38.1 0.6 outside0.1
  38.7 0.9 %collective-permute-done.2.refs_0_ = bf16[272,256]{1,0:T(8,128)(2,1)S(1)} collective-permute-done((bf16[272,256]{1,0:T(8,128)(2,1)S(1)}, bf16[272,256]{1,0:T(8,128)(2,1)S(1)}, u32[]{:S(2)}, u32[]{:S(2)}) %collective-permute-start.2) | collective-permute-done | bytes 139296 | tf_op jit(solution)/shard_map/ppermute | solution.py:338
  39.6 1.4 %outside1.1 = (bf16[512,256]{1,0:T(8,128)(2,1)S(1)}, bf16[384,256]{1,0:T(8,128)(2,1)S(1)}, bf16[128,256]{1,0:T(8,128)(2,1)S(1)}) custom-call(bf16[272,256]{1,0:T(8,128)(2,1)S(1)} %collective-permute-done.2.refs_0_, f32[4,64,256]{2,1,0:T(8,128)S(1)} %get-tuple-element.67.refs_1_, f32[8,256]{1,0:T(8,128)S(1)} %get-tuple-element.68.refs_2_, ...), custom_call_target="tpu_custom_call" | custom-call | tf_op jit(solution)/shard_map/outside1/pallas_call | solution.py:490
  40.9 0.6 collective-permute-start.6
  41.6 5.1 %collective-permute-done.6.refs_0_ = bf16[384,256]{1,0:T(8,128)(2,1)S(1)} collective-permute-done((bf16[384,256]{1,0:T(8,128)(2,1)S(1)}, bf16[384,256]{1,0:T(8,128)(2,1)S(1)}, u32[]{:S(2)}, u32[]{:S(2)}) %collective-permute-start.6) | collective-permute-done | bytes 196640 | tf_op jit(solution)/shard_map/ppermute | solution.py:338
  46.7 0.0 collective-permute-start.7
  46.7 2.4 %fetch.1 = (bf16[256,1024]{1,0:T(8,128)(2,1)S(1)}, bf16[1024,1024]{1,0:T(8,128)(2,1)S(1)}, bf16[1024,1024]{1,0:T(8,128)(2,1)S(1)}, f32[1,1024]{1,0:T(1,128)S(1)}) custom-call(bf16[256,1024]{1,0:T(8,128)(2,1)} %refs_0_.1, bf16[1024,1024]{1,0:T(8,128)(2,1)} %refs_1_.1, bf16[1024,1024]{1,0:T(8,128)(2,1)} %refs_2_.1, bf16[1024]{0:T(1024)(128)(2,1)} %refs_3_.1), custom_call_target="tpu_custom_call" | custom-call | tf_op jit(solution)/shard_map/fetch/pallas_call | solution.py:500
  49.1 0.0 collective-permute-done.10.near
  49.2 0.7 %own.1.refs_4_ = f32[512,1024]{1,0:T(8,128)S(1)} custom-call(bf16[512,256]{1,0:T(8,128)(2,1)S(1)} %get-tuple-element.90.mine, bf16[512,256]{1,0:T(8,128)(2,1)S(1)} %collective-permute-done.10.near, bf16[256,1024]{1,0:T(8,128)(2,1)S(1)} %get-tuple-element.91.own_w, bf16[256,1024]{1,0:T(8,128)(2,1)S(1)} %collective-permute-done.11.near_w, ...), custom_call_target="tpu_custom_call" | custom-call | tf_op jit(solution)/shard_map/own/pallas_call | solution.py:517
  49.9 0.0 collective-permute-done.7.refs_1_
  49.9 0.0 collective-permute-done.9.refs_3_
  49.9 2.6 %shard_map.140 = (f32[384,256]{1,0:T(8,128)S(1)}, f32[384,256]{1,0:T(8,128)S(1)}, bf16[384,512]{1,0:T(8,128)(2,1)S(1)}) custom-call(bf16[384,256]{1,0:T(8,128)(2,1)S(1)} %collective-permute-done.6.refs_0_, bf16[384,256]{1,0:T(8,128)(2,1)S(1)} %collective-permute-done.7.refs_1_, bf16[256,1024]{1,0:T(8,128)(2,1)S(1)} %collective-permute-done.8.refs_2_, ...), custom_call_target="tpu_custom_call" | custom-call | tf_op jit(solution)/shard_map/pallas_call | solution.py:527
  52.5 0.6 collective-permute-start.12
  53.0 0.5 collective-permute-start.14
  53.6 3.7 %collective-permute-done.14.refs_0_ = bf16[128,256]{1,0:T(8,128)(2,1)S(1)} collective-permute-done((bf16[128,256]{1,0:T(8,128)(2,1)S(1)}, bf16[128,256]{1,0:T(8,128)(2,1)S(1)}, u32[]{:S(2)}, u32[]{:S(2)}) %collective-permute-start.14) | collective-permute-done | bytes 65568 | tf_op jit(solution)/shard_map/ppermute | solution.py:338
  57.3 1.3 %collective-permute-done.15.refs_1_ = bf16[128,256]{1,0:T(8,128)(2,1)S(1)} collective-permute-done((bf16[128,256]{1,0:T(8,128)(2,1)S(1)}, bf16[128,256]{1,0:T(8,128)(2,1)S(1)}, u32[]{:S(2)}, u32[]{:S(2)}) %collective-permute-start.15) | collective-permute-done | bytes 65568 | tf_op jit(solution)/shard_map/ppermute | solution.py:338
  58.6 1.2 %shard_map.141 = (f32[128,256]{1,0:T(8,128)S(1)}, f32[128,256]{1,0:T(8,128)S(1)}, bf16[128,512]{1,0:T(8,128)(2,1)S(1)}) custom-call(bf16[128,256]{1,0:T(8,128)(2,1)S(1)} %collective-permute-done.14.refs_0_, bf16[128,256]{1,0:T(8,128)(2,1)S(1)} %collective-permute-done.15.refs_1_, bf16[256,1024]{1,0:T(8,128)(2,1)S(1)} %collective-permute-done.8.refs_2_, ...), custom_call_target="tpu_custom_call" | custom-call | tf_op jit(solution)/shard_map/pallas_call | solution.py:527
  59.8 0.2 collective-permute-start.16
  60.1 0.6 collective-permute-start.13
  60.7 0.5 collective-permute-done.16.refs_4_
  61.2 1.0 %collective-permute-start.17 = (bf16[128,256]{1,0:T(8,128)(2,1)S(1)}, bf16[128,256]{1,0:T(8,128)(2,1)S(1)}, u32[]{:S(2)}, u32[]{:S(2)}) collective-permute-start(bf16[128,256]{1,0:T(8,128)(2,1)S(1)} %add_convert_fusion.1), channel_id=1, source_target_pairs={{0,2},{1,3},{2,0},{3,1},{4,6},{5,7},{6,4},{7,5},{8,10},{9,11},{10,... | collective-permute-start | bytes 196616 | tf_op jit(solution)/shard_map/ppermute | solution.py:338
  62.2 6.5 %collective-permute-done.17.refs_5_ = bf16[128,256]{1,0:T(8,128)(2,1)S(1)} collective-permute-done((bf16[128,256]{1,0:T(8,128)(2,1)S(1)}, bf16[128,256]{1,0:T(8,128)(2,1)S(1)}, u32[]{:S(2)}, u32[]{:S(2)}) %collective-permute-start.17) | collective-permute-done | bytes 65568 | tf_op jit(solution)/shard_map/ppermute | solution.py:338
  68.7 0.0 collective-permute-done.13.refs_2_
  68.7 0.8 %final.1 = bf16[512,256]{1,0:T(8,128)(2,1)} custom-call(f32[384,256]{1,0:T(8,128)S(1)} %get-tuple-element.96.refs_0_, bf16[384,512]{1,0:T(8,128)(2,1)S(1)} %collective-permute-done.12.refs_1_, bf16[384,256]{1,0:T(8,128)(2,1)S(1)} %collective-permute-done.13.refs_2_, f32[128,256]{1,0:T(8,128)S(1)} %get-tuple-element.100.refs_3_, ...), custom_call_target="tpu_custom_call" | custom-call | tf_op jit(solution)/shard_map/final/pallas_call | solution.py:550
  (11 shorter events, 0.1 us)
Async XLA Ops:
  0.0 34.1 %collective-permute-start.8 = (bf16[256,1024]{1,0:T(8,128)(2,1)}, bf16[256,1024]{1,0:T(8,128)(2,1)S(1)}, u32[]{:S(2)}, u32[]{:S(2)}) collective-permute-start(bf16[256,1024]{1,0:T(8,128)(2,1)} %refs_0_.1), channel_id=1, source_target_pairs={{0,2},{1,3},{2,0},{3,1},{4,6},{5,7},{6,4},{7,5},{8,10},{9,11},{10,... | collective-permute-start | bytes 1572872 | tf_op jit(solution)/shard_map/ppermute | solution.py:338
  3.0 12.4 %all-to-all-start = ((f32[8,4,128]{2,1,0:T(4,128)}), f32[8,4,128]{2,1,0:T(4,128)S(1)}, u32[]{:S(2)}, u32[]{:S(2)}) async-start(f32[8,4,128]{2,1,0:T(4,128)} %bitcast.5), calls=%async_computation | async-start | bytes 32768 | tf_op jit(solution)/shard_map/all_to_all | solution.py:365
  13.0 21.6 %copy-start.1 = (bf16[256]{0:T(256)(128)(2,1)S(1)}, bf16[256]{0:T(256)(128)(2,1)}, u32[]{:S(2)}) copy-start(bf16[256]{0:T(256)(128)(2,1)} %param.23) | copy-start | bytes 1540
  15.4 18.7 %copy-start = (bf16[256,1024]{1,0:T(8,128)(2,1)S(1)}, bf16[256,1024]{1,0:T(8,128)(2,1)}, u32[]{:S(2)}) copy-start(bf16[256,1024]{1,0:T(8,128)(2,1)} %refs_0_.1) | copy-start | bytes 1572868
  17.5 5.3 %collective-permute-start.3 = (bf16[272,256]{1,0:T(8,128)(2,1)S(1)}, bf16[272,256]{1,0:T(8,128)(2,1)S(1)}, u32[]{:S(2)}, u32[]{:S(2)}) collective-permute-start(bf16[272,256]{1,0:T(8,128)(2,1)S(1)} %get-tuple-element.72), channel_id=1, source_target_pairs={{0,4},{4,0},{8,12},{12,8},{16,20},{20,16},{24,28},{28,24},{1,5},{5... | collective-permute-start | bytes 417800 | tf_op jit(solution)/shard_map/ppermute | solution.py:338
  18.1 6.2 %collective-permute-start = (bf16[272,256]{1,0:T(8,128)(2,1)S(1)}, bf16[272,256]{1,0:T(8,128)(2,1)S(1)}, u32[]{:S(2)}, u32[]{:S(2)}) collective-permute-start(bf16[272,256]{1,0:T(8,128)(2,1)S(1)} %get-tuple-element.58), channel_id=1, source_target_pairs={{0,4},{4,0},{8,12},{12,8},{16,20},{20,16},{24,28},{28,24},{1,5},{5... | collective-permute-start | bytes 417800 | tf_op jit(solution)/shard_map/ppermute | solution.py:338
  22.9 5.5 %collective-permute-start.4 = (bf16[272,256]{1,0:T(8,128)(2,1)S(1)}, bf16[272,256]{1,0:T(8,128)(2,1)S(1)}, u32[]{:S(2)}, u32[]{:S(2)}) collective-permute-start(bf16[272,256]{1,0:T(8,128)(2,1)S(1)} %get-tuple-element.75), channel_id=1, source_target_pairs={{0,8},{4,12},{8,0},{12,4},{16,24},{20,28},{24,16},{28,20},{1,9},{5... | collective-permute-start | bytes 417800 | tf_op jit(solution)/shard_map/ppermute | solution.py:338
  24.4 7.0 %collective-permute-start.1 = (bf16[272,256]{1,0:T(8,128)(2,1)S(1)}, bf16[272,256]{1,0:T(8,128)(2,1)S(1)}, u32[]{:S(2)}, u32[]{:S(2)}) collective-permute-start(bf16[272,256]{1,0:T(8,128)(2,1)S(1)} %get-tuple-element.61), channel_id=1, source_target_pairs={{0,8},{4,12},{8,0},{12,4},{16,24},{20,28},{24,16},{28,20},{1,9},{5... | collective-permute-start | bytes 417800 | tf_op jit(solution)/shard_map/ppermute | solution.py:338
  28.5 9.6 %collective-permute-start.5 = (bf16[272,256]{1,0:T(8,128)(2,1)S(1)}, bf16[272,256]{1,0:T(8,128)(2,1)S(1)}, u32[]{:S(2)}, u32[]{:S(2)}) collective-permute-start(bf16[272,256]{1,0:T(8,128)(2,1)S(1)} %get-tuple-element.80), channel_id=1, source_target_pairs={{0,16},{4,20},{8,24},{12,28},{16,0},{20,4},{24,8},{28,12},{1,17},{... | collective-permute-start | bytes 417800 | tf_op jit(solution)/shard_map/ppermute | solution.py:338
  31.5 8.1 %collective-permute-start.2 = (bf16[272,256]{1,0:T(8,128)(2,1)S(1)}, bf16[272,256]{1,0:T(8,128)(2,1)S(1)}, u32[]{:S(2)}, u32[]{:S(2)}) collective-permute-start(bf16[272,256]{1,0:T(8,128)(2,1)S(1)} %get-tuple-element.66), channel_id=1, source_target_pairs={{0,16},{4,20},{8,24},{12,28},{16,0},{20,4},{24,8},{28,12},{1,17},{... | collective-permute-start | bytes 417800 | tf_op jit(solution)/shard_map/ppermute | solution.py:338
  34.1 15.1 %collective-permute-start.11 = (bf16[256,1024]{1,0:T(8,128)(2,1)S(1)}, bf16[256,1024]{1,0:T(8,128)(2,1)S(1)}, u32[]{:S(2)}, u32[]{:S(2)}) collective-permute-start(bf16[256,1024]{1,0:T(8,128)(2,1)S(1)} %copy-done), channel_id=1, source_target_pairs={{0,1},{1,0},{2,3},{3,2},{4,5},{5,4},{6,7},{7,6},{8,9},{9,8},{10,11... | collective-permute-start | bytes 1572872 | tf_op jit(solution)/shard_map/ppermute | solution.py:338
  34.1 15.8 %collective-permute-start.9 = (bf16[256,1024]{1,0:T(8,128)(2,1)S(1)}, bf16[256,1024]{1,0:T(8,128)(2,1)S(1)}, u32[]{:S(2)}, u32[]{:S(2)}) collective-permute-start(bf16[256,1024]{1,0:T(8,128)(2,1)S(1)} %collective-permute-done.8.refs_2_), channel_id=1, source_target_pairs={{0,1},{1,0},{2,3},{3,2},{4,5},{5,4},{6,7},{7,6},{8,9},{9,8},{10,11... | collective-permute-start | bytes 1572872 | tf_op jit(solution)/shard_map/ppermute | solution.py:338
  40.9 5.7 %collective-permute-start.6 = (bf16[384,256]{1,0:T(8,128)(2,1)S(1)}, bf16[384,256]{1,0:T(8,128)(2,1)S(1)}, u32[]{:S(2)}, u32[]{:S(2)}) collective-permute-start(bf16[384,256]{1,0:T(8,128)(2,1)S(1)} %get-tuple-element.89), channel_id=1, source_target_pairs={{0,2},{1,3},{2,0},{3,1},{4,6},{5,7},{6,4},{7,5},{8,10},{9,11},{10,... | collective-permute-start | bytes 589832 | tf_op jit(solution)/shard_map/ppermute | solution.py:338
  41.5 7.6 %collective-permute-start.10 = (bf16[512,256]{1,0:T(8,128)(2,1)S(1)}, bf16[512,256]{1,0:T(8,128)(2,1)S(1)}, u32[]{:S(2)}, u32[]{:S(2)}) collective-permute-start(bf16[512,256]{1,0:T(8,128)(2,1)S(1)} %get-tuple-element.90.mine), channel_id=1, source_target_pairs={{0,1},{1,0},{2,3},{3,2},{4,5},{5,4},{6,7},{7,6},{8,9},{9,8},{10,11... | collective-permute-start | bytes 786440 | tf_op jit(solution)/shard_map/ppermute | solution.py:338
  46.7 3.2 %collective-permute-start.7 = (bf16[384,256]{1,0:T(8,128)(2,1)S(1)}, bf16[384,256]{1,0:T(8,128)(2,1)S(1)}, u32[]{:S(2)}, u32[]{:S(2)}) collective-permute-start(bf16[384,256]{1,0:T(8,128)(2,1)S(1)} %collective-permute-done.6.refs_0_), channel_id=1, source_target_pairs={{0,1},{1,0},{2,3},{3,2},{4,5},{5,4},{6,7},{7,6},{8,9},{9,8},{10,11... | collective-permute-start | bytes 589832 | tf_op jit(solution)/shard_map/ppermute | solution.py:338
  52.5 7.5 %collective-permute-start.12 = (bf16[384,512]{1,0:T(8,128)(2,1)S(1)}, bf16[384,512]{1,0:T(8,128)(2,1)S(1)}, u32[]{:S(2)}, u32[]{:S(2)}) collective-permute-start(bf16[384,512]{1,0:T(8,128)(2,1)S(1)} %get-tuple-element.97), channel_id=1, source_target_pairs={{0,1},{1,0},{2,3},{3,2},{4,5},{5,4},{6,7},{7,6},{8,9},{9,8},{10,11... | collective-permute-start | bytes 1179656 | tf_op jit(solution)/shard_map/ppermute | solution.py:338
  53.0 4.3 %collective-permute-start.14 = (bf16[128,256]{1,0:T(8,128)(2,1)S(1)}, bf16[128,256]{1,0:T(8,128)(2,1)S(1)}, u32[]{:S(2)}, u32[]{:S(2)}) collective-permute-start(bf16[128,256]{1,0:T(8,128)(2,1)S(1)} %get-tuple-element.99), channel_id=1, source_target_pairs={{0,2},{1,3},{2,0},{3,1},{4,6},{5,7},{6,4},{7,5},{8,10},{9,11},{10,... | collective-permute-start | bytes 196616 | tf_op jit(solution)/shard_map/ppermute | solution.py:338
  57.3 1.3 %collective-permute-start.15 = (bf16[128,256]{1,0:T(8,128)(2,1)S(1)}, bf16[128,256]{1,0:T(8,128)(2,1)S(1)}, u32[]{:S(2)}, u32[]{:S(2)}) collective-permute-start(bf16[128,256]{1,0:T(8,128)(2,1)S(1)} %collective-permute-done.14.refs_0_), channel_id=1, source_target_pairs={{0,1},{1,0},{2,3},{3,2},{4,5},{5,4},{6,7},{7,6},{8,9},{9,8},{10,11... | collective-permute-start | bytes 196616 | tf_op jit(solution)/shard_map/ppermute | solution.py:338
  59.8 1.4 %collective-permute-start.16 = (bf16[128,512]{1,0:T(8,128)(2,1)S(1)}, bf16[128,512]{1,0:T(8,128)(2,1)S(1)}, u32[]{:S(2)}, u32[]{:S(2)}) collective-permute-start(bf16[128,512]{1,0:T(8,128)(2,1)S(1)} %get-tuple-element.101), channel_id=1, source_target_pairs={{0,1},{1,0},{2,3},{3,2},{4,5},{5,4},{6,7},{7,6},{8,9},{9,8},{10,11... | collective-permute-start | bytes 393224 | tf_op jit(solution)/shard_map/ppermute | solution.py:338
  60.1 8.6 %collective-permute-start.13 = (bf16[384,256]{1,0:T(8,128)(2,1)S(1)}, bf16[384,256]{1,0:T(8,128)(2,1)S(1)}, u32[]{:S(2)}, u32[]{:S(2)}) collective-permute-start(bf16[384,256]{1,0:T(8,128)(2,1)S(1)} %add_convert_fusion), channel_id=1, source_target_pairs={{0,2},{1,3},{2,0},{3,1},{4,6},{5,7},{6,4},{7,5},{8,10},{9,11},{10,... | collective-permute-start | bytes 589832 | tf_op jit(solution)/shard_map/ppermute | solution.py:338
  61.2 7.5 %collective-permute-start.17 = (bf16[128,256]{1,0:T(8,128)(2,1)S(1)}, bf16[128,256]{1,0:T(8,128)(2,1)S(1)}, u32[]{:S(2)}, u32[]{:S(2)}) collective-permute-start(bf16[128,256]{1,0:T(8,128)(2,1)S(1)} %add_convert_fusion.1), channel_id=1, source_target_pairs={{0,2},{1,3},{2,0},{3,1},{4,6},{5,7},{6,4},{7,5},{8,10},{9,11},{10,... | collective-permute-start | bytes 196616 | tf_op jit(solution)/shard_map/ppermute | solution.py:338
